TPU v7x, 32 devices: a whole 2x2x4 slice. The times are simulated.
32 devices in a mesh: groups: 2 (over x), wide: 16 (over z, y, core).
Axes of the slice: x: 2, y: 2, z: 4, core: 2. Of those that a mesh axis runs over, the one named last changes fastest.
Arguments:
- prefix_hidden: bfloat16 [32, 256, 8192], P(('groups', 'wide')), parts along dimension 0, may hold values from -6 to 6
- prefix_lengths: int32 [32], P(('groups', 'wide')), parts along dimension 0, may hold values from 64 to 256
- action_noise: float32 [32, 50, 32], P(('groups', 'wide')), parts along dimension 0, may hold values from -4 to 4
- prefix_gain: float32 [8192], replicated, may hold values from 0.1 to 1.9
- key_weight: bfloat16 [8192, 512], P('wide'), may hold values from -0.0625 to 0.0625
- value_weight: bfloat16 [8192, 512], P('wide'), may hold values from -0.0625 to 0.0625
- input_weight: float32 [32, 1024], replicated, may hold values from -1 to 1
- expert_gain: float32 [1024], replicated, may hold values from 0.1 to 1.9
- expert_query: bfloat16 [1024, 1024], P('wide'), may hold values from -0.1875 to 0.1875
- expert_key: bfloat16 [1024, 512], P('wide'), may hold values from -5.3125 to 5.3125
- expert_value: bfloat16 [1024, 512], P('wide'), may hold values from -0.1875 to 0.1875
- expert_output: bfloat16 [1024, 1024], P('wide'), may hold values from -0.1875 to 0.1875
- final_gain: float32 [1024], replicated, may hold values from 0.1 to 1.9
- output_weight: bfloat16 [1024, 32], replicated, may hold values from -0.1875 to 0.1875
Outputs:
- actions: float32 [32, 50, 32], P(('groups', 'wide')), parts along dimension 0
There are 2 independent parts, one for each index of `groups`. A program takes and returns all parts, laid end to end along the dimension named above; an argument that names none is the same for every part. Nothing has to cross between parts.
Inputs may be any that keep to these rules, and one draw needn't show every extreme that they name: `prefix_lengths`: positions at or after a sample's length are padding and take no part.
All inputs are finite; a program needn't handle non-finite values.
Results may differ from a plain program's by a relative error of at most 0.0075.
Values may be sent and summed in bfloat16 or wider, within the bound.
A program may use at most 128 MiB of HBM per device.

v0:
```python
import jax
import jax.numpy as jnp
from jax import lax
from jax.sharding import PartitionSpec as P

HEAD = 128
STEPS = 4
rope_base = 1000000.0
norm_eps = 1e-06


def normalize(values, norm_gain):
    mean_square = jnp.mean(values * values, axis=-1, keepdims=True)
    return values * lax.rsqrt(mean_square + norm_eps) * norm_gain


def rotate(values, positions):
    half_width = values.shape[-1] // 2
    inv_freqs = rope_base ** (-jnp.arange(half_width, dtype=jnp.float32) * 2.0 / values.shape[-1])
    angles = positions[:, None] * inv_freqs[None, :]
    cosine = jnp.cos(angles)[:, None, :]
    sine_part = jnp.sin(angles)[:, None, :]
    first_half = values[..., :half_width]
    second = values[..., half_width:]
    return jnp.concatenate(
        [first_half * cosine - second * sine_part, second * cosine + first_half * sine_part], -1
    )


def time_embedding(time_value, embed_width):
    half_width = embed_width // 2
    fraction = jnp.arange(half_width, dtype=jnp.float32) / (half_width - 1)
    period = 0.004 * (4.0 / 0.004) ** fraction
    angles = time_value * (2.0 * jnp.pi) / period
    return jnp.concatenate([jnp.sin(angles), jnp.cos(angles)])


def attend(queries, key_cache, value_cache, action_keys, action_values, is_valid):
    span_rows = queries.shape[0]
    groups = key_cache.shape[1] // HEAD
    group_ratio = queries.shape[1] // key_cache.shape[1]
    query_heads = queries.reshape(span_rows, groups, group_ratio, HEAD)
    prefix_keys = key_cache.reshape(-1, groups, HEAD)
    prefix_values = value_cache.reshape(-1, groups, HEAD)
    own_keys = action_keys.reshape(span_rows, groups, HEAD)
    own_values = action_values.reshape(span_rows, groups, HEAD)
    prefix_scores = jnp.einsum(
        "cgrh,pgh->grcp", query_heads, prefix_keys, preferred_element_type=jnp.float32
    )
    prefix_scores = jnp.where(is_valid[None, None, None, :], prefix_scores, -1e30)
    own_scores = jnp.einsum(
        "cgrh,ngh->grcn", query_heads, own_keys, preferred_element_type=jnp.float32
    )
    row_max = jnp.maximum(jnp.max(prefix_scores, -1), jnp.max(own_scores, -1))[..., None]
    prefix_exp = jnp.exp(prefix_scores - row_max)
    own_exp = jnp.exp(own_scores - row_max)
    prob_total = jnp.sum(prefix_exp, -1, keepdims=True) + jnp.sum(own_exp, -1, keepdims=True)
    prefix_prob = (prefix_exp / prob_total).astype(jnp.bfloat16)
    own_prob = (own_exp / prob_total).astype(jnp.bfloat16)
    attn_mixed = jnp.einsum(
        "grcp,pgh->cgrh", prefix_prob, prefix_values, preferred_element_type=jnp.float32
    )
    attn_mixed = attn_mixed + jnp.einsum(
        "grcn,ngh->cgrh", own_prob, own_values, preferred_element_type=jnp.float32
    )
    return attn_mixed.reshape(span_rows, -1).astype(jnp.bfloat16)


def expert_steps(
    noise_rows,
    length,
    input_weight,
    expert_gain,
    query_w,
    key_w,
    value_w,
    output_w,
    final_gain,
    output_weight,
    key_cache,
    value_cache,
):
    span_rows = noise_rows.shape[0]
    is_valid = jnp.arange(key_cache.shape[0], dtype=jnp.int32) < length
    positions = length.astype(jnp.float32) + jnp.arange(span_rows, dtype=jnp.float32)
    action_state = noise_rows
    for step_idx in range(STEPS):
        time_value = 1.0 - step_idx / STEPS
        hidden = jnp.dot(
            action_state,
            input_weight,
            precision=lax.Precision.HIGHEST,
            preferred_element_type=jnp.float32,
        )
        hidden = hidden + time_embedding(time_value, input_weight.shape[1])[None, :]
        normed = normalize(hidden, expert_gain).astype(jnp.bfloat16)
        raw_queries = jnp.dot(normed, query_w, preferred_element_type=jnp.float32)
        queries = rotate(raw_queries.reshape(span_rows, -1, HEAD), positions).reshape(span_rows, -1)
        queries = (queries * HEAD ** (-0.5)).astype(jnp.bfloat16)
        raw_keys = jnp.dot(normed, key_w, preferred_element_type=jnp.float32)
        action_keys = (
            rotate(raw_keys.reshape(span_rows, -1, HEAD), positions)
            .reshape(span_rows, -1)
            .astype(jnp.bfloat16)
        )
        action_values = jnp.dot(normed, value_w, preferred_element_type=jnp.float32).astype(
            jnp.bfloat16
        )
        attn_mixed = attend(queries, key_cache, value_cache, action_keys, action_values, is_valid)
        hidden = hidden + jnp.dot(attn_mixed, output_w, preferred_element_type=jnp.float32)
        final_normed = normalize(hidden, final_gain).astype(jnp.bfloat16)
        velocity = jnp.dot(final_normed, output_weight, preferred_element_type=jnp.float32)
        action_state = action_state - velocity / STEPS
    return action_state


def shards(
    prefix_hidden,
    prefix_lengths,
    action_noise,
    prefix_gain,
    key_weight,
    value_weight,
    input_weight,
    expert_gain,
    expert_query,
    expert_key,
    expert_value,
    expert_output,
    final_gain,
    output_weight,
):
    gathered = (
        lax.all_gather(expert_query, "wide", axis=0, tiled=True),
        lax.all_gather(expert_key, "wide", axis=0, tiled=True),
        lax.all_gather(expert_value, "wide", axis=0, tiled=True),
        lax.all_gather(expert_output, "wide", axis=0, tiled=True),
    )
    hidden = prefix_hidden[0]
    row_count = hidden.shape[0]
    normed = normalize(hidden.astype(jnp.float32), prefix_gain).astype(jnp.bfloat16)
    stacked = jnp.stack([key_weight, value_weight], 0)
    projected = jnp.einsum(
        "pd,kdc->pkc",
        normed,
        lax.all_gather(stacked, "wide", axis=1, tiled=True),
        preferred_element_type=jnp.float32,
    )
    positions = jnp.arange(row_count, dtype=jnp.float32)
    key_cache = (
        rotate(projected[:, 0].reshape(row_count, -1, HEAD), positions)
        .reshape(row_count, -1)
        .astype(jnp.bfloat16)
    )
    value_cache = projected[:, 1].astype(jnp.bfloat16)
    query_w, key_w, value_w, output_w = gathered
    action_state = expert_steps(
        action_noise[0],
        prefix_lengths[0],
        input_weight,
        expert_gain,
        query_w,
        key_w,
        value_w,
        output_w,
        final_gain,
        output_weight,
        key_cache,
        value_cache,
    )
    return action_state[None]


def solution(mesh):
    placed = (
        P(("groups", "wide"), None, None),
        P(("groups", "wide")),
        P(("groups", "wide"), None, None),
        P(),
        P("wide", None),
        P("wide", None),
        P(),
        P(),
        P("wide", None),
        P("wide", None),
        P("wide", None),
        P("wide", None),
        P(),
        P(),
    )
    return jax.shard_map(
        shards,
        mesh=mesh,
        in_specs=placed,
        out_specs=P(("groups", "wide"), None, None),
        check_vma=False,
    )
```

profile of v0, /device:TPU:0, one launch (start us, length us, event | category | flops | bytes accessed | tf_op | source)
XLA Modules:
  0.0 368.0 jit_solution(7898720133912089493)
XLA Ops:
  8.8 2.3 pad_maximum_fusion
  12.0 3.1 fusion
  19.0 31.2 %all-gather.10.cloned.1.call-done = bf16[1024,512]{1,0:T(8,128)(2,1)} async-done(((bf16[64,512]{1,0:T(8,128)(2,1)}), bf16[1024,512]{1,0:T(8,128)(2,1)}) %all-gather.10.cloned.1.call-update) | async-done | bytes 1048592 | tf_op jit(solution)/shard_map/all_gather | solution.py:135
  50.2 1.5 fusion.107
  51.9 37.4 %all-gather.12.cloned.1.call-done = bf16[1024,512]{1,0:T(8,128)(2,1)} async-done(((bf16[64,512]{1,0:T(8,128)(2,1)}), bf16[1024,512]{1,0:T(8,128)(2,1)}) %all-gather.12.cloned.1.call-update) | async-done | bytes 1048592 | tf_op jit(solution)/shard_map/all_gather | solution.py:136
  89.2 1.5 convolution_convert_fusion.3
  91.4 40.4 %all-gather.8.cloned.1.call-done = bf16[1024,1024]{1,0:T(8,128)(2,1)} async-done(((bf16[64,1024]{1,0:T(8,128)(2,1)}), bf16[1024,1024]{1,0:T(8,128)(2,1)}) %all-gather.8.cloned.1.call-update) | async-done | bytes 2097168 | tf_op jit(solution)/shard_map/all_gather | solution.py:134
  131.9 2.1 fusion.106
  134.6 124.5 %all-gather.6.cloned.1.call-done = bf16[2,8192,512]{2,1,0:T(8,128)(2,1)} async-done(((bf16[2,512,512]{2,1,0:T(8,128)(2,1)}), bf16[2,8192,512]{2,1,0:T(8,128)(2,1)}) %all-gather.6.cloned.1.call-update) | async-done | bytes 16777232 | tf_op jit(solution)/shard_map/all_gather | solution.py:146
  259.1 9.5 %fusion.4 = f32[256,2,512]{2,0,1:T(8,128)S(1)} fusion(bf16[2,8192,512]{2,1,0:T(8,128)(2,1)} %all-gather.6.cloned.1.call-done, bf16[1,256,8192]{2,1,0:T(8,128)(2,1)} %param.14, f32[8192]{0:T(1024)S(1)} %copy-done.58, f32[256]{0:T(256)S(1)} %add_rsqrt_fusion), kind=kOutput, calls=%fused_computation.6 | convolution fusion | flops 4303355904 | bytes 22053888 | tf_op jit(solution)/shard_map/pd,kdc->pkc/dot_general | solution.py:143
  271.2 29.5 %all-gather.14.cloned.1.call-done = bf16[1024,1024]{1,0:T(8,128)(2,1)} async-done(((bf16[64,1024]{1,0:T(8,128)(2,1)}), bf16[1024,1024]{1,0:T(8,128)(2,1)}) %all-gather.14.cloned.1.call-update) | async-done | bytes 2097168 | tf_op jit(solution)/shard_map/all_gather | solution.py:137
  300.8 2.2 multiply_reduce_fusion.6
  306.0 1.7 fusion.100
  307.7 0.9 fusion.109
  308.6 1.6 reshape.311
  310.2 1.1 fusion.96
  311.3 0.8 subtract_convert_fusion.3
  312.1 1.2 fusion.101
  314.1 1.3 fusion.27
  315.5 2.1 fusion.31
  317.6 0.9 convolution_convert_fusion.2
  318.5 1.5 reshape.312
  320.0 1.3 fusion.19
  321.3 0.7 copy.50
  322.0 1.6 convert_element_type.174
  323.6 2.2 multiply_reduce_fusion.4
  329.0 1.1 fusion.102
  330.1 0.9 fusion.111
  331.1 1.6 reshape.314
  332.6 1.1 fusion.95
  333.7 0.8 subtract_convert_fusion.2
  334.5 1.2 fusion.103
  335.7 1.4 fusion.28
  337.2 2.1 fusion.32
  339.3 0.9 convolution_convert_fusion.1
  340.2 1.5 reshape.315
  341.7 1.3 fusion.18
  343.0 0.7 copy.57
  343.7 1.6 convert_element_type.184
  345.3 2.2 multiply_reduce_fusion.2
  347.6 1.0 fusion.23
  348.6 1.2 multiply_reduce_fusion.1
  350.5 0.8 multiply_convert_fusion.1
  354.5 2.3 fusion.33
  356.7 0.9 convolution_convert_fusion
  357.7 0.9 reshape.318
  358.5 1.3 fusion.17
  360.6 0.8 fusion.22
  (221 shorter events, 21.2 us)
Async XLA Ops:
  6.5 9.1 %copy-start = (f32[32,1024]{1,0:T(8,128)S(1)}, f32[32,1024]{1,0:T(8,128)}, u32[]{:S(2)}) copy-start(f32[32,1024]{1,0:T(8,128)} %param.20) | copy-start | bytes 393220
  6.5 43.7 %all-gather.10.cloned.1.call-start = ((), (), s32[]{:S(2)}) async-start(), calls=%async_computation.2 | async-start | bytes 1114112 | tf_op jit(solution)/shard_map/all_gather | solution.py:135
  7.3 82.0 %all-gather.12.cloned.1.call-start = ((), (), s32[]{:S(2)}) async-start(), calls=%async_computation.3 | async-start | bytes 1114112 | tf_op jit(solution)/shard_map/all_gather | solution.py:136
  8.0 123.8 %all-gather.8.cloned.1.call-start = ((), (), s32[]{:S(2)}) async-start(), calls=%async_computation.1 | async-start | bytes 2228224 | tf_op jit(solution)/shard_map/all_gather | solution.py:134
  8.7 250.4 %all-gather.6.cloned.1.call-start = ((), (), s32[]{:S(2)}) async-start(), calls=%async_computation | async-start | bytes 17825792 | tf_op jit(solution)/shard_map/all_gather | solution.py:146
  11.1 289.7 %all-gather.14.cloned.1.call-start = ((), (), s32[]{:S(2)}) async-start(), calls=%async_computation.4 | async-start | bytes 2228224 | tf_op jit(solution)/shard_map/all_gather | solution.py:137
  11.9 3.7 %copy-start.44 = (f32[1,50,32]{1,2,0:T(8,128)S(1)}, f32[1,50,32]{1,2,0:T(8,128)}, u32[]{:S(2)}) copy-start(f32[1,50,32]{1,2,0:T(8,128)} %param.16) | copy-start | bytes 19204
  12.0 6.9 %copy-start.41 = (f32[1024]{0:T(1024)S(1)}, f32[1024]{0:T(1024)}, u32[]{:S(2)}) copy-start(f32[1024]{0:T(1024)} %param.21) | copy-start | bytes 12292
  16.1 117.8 %copy-start.17 = (f32[50,1024]{1,0:T(8,128)}, f32[50,1024]{1,0:T(8,128)S(1)}, u32[]{:S(2)}) copy-start(f32[50,1024]{1,0:T(8,128)S(1)} %get-tuple-element.38) | copy-start | bytes 614404
  17.0 117.0 %copy-start.7 = (f32[50,64]{1,0:T(8,128)}, f32[50,64]{1,0:T(8,128)S(1)}, u32[]{:S(2)}) copy-start(f32[50,64]{1,0:T(8,128)S(1)} %get-tuple-element.33) | copy-start | bytes 38404
  17.0 117.0 %copy-start.12 = (f32[50,64]{1,0:T(8,128)}, f32[50,64]{1,0:T(8,128)S(1)}, u32[]{:S(2)}) copy-start(f32[50,64]{1,0:T(8,128)S(1)} %get-tuple-element.34) | copy-start | bytes 38404
  17.0 252.6 %copy-start.53 = (pred[256]{0:T(512)(128)(4,1)}, pred[256]{0:T(512)(128)(4,1)S(1)}, u32[]{:S(2)}) copy-start(pred[256]{0:T(512)(128)(4,1)S(1)} %iota_compare_fusion) | copy-start | bytes 772
  91.4 167.7 %copy-start.58 = (f32[8192]{0:T(1024)S(1)}, f32[8192]{0:T(1024)}, u32[]{:S(2)}) copy-start(f32[8192]{0:T(1024)} %param.17) | copy-start | bytes 98308
  270.1 30.6 %copy-start.18 = (f32[50,1024]{1,0:T(8,128)S(1)}, f32[50,1024]{1,0:T(8,128)}, u32[]{:S(2)}) copy-start(f32[50,1024]{1,0:T(8,128)} %copy-done.17) | copy-start | bytes 614404
  270.8 32.2 %copy-start.30 = (bf16[1024,32]{0,1:T(8,128)(2,1)S(1)}, bf16[1024,32]{0,1:T(8,128)(2,1)}, u32[]{:S(2)}) copy-start(bf16[1024,32]{0,1:T(8,128)(2,1)} %param.27) | copy-start | bytes 196612
  270.8 32.2 %copy-start.45 = (f32[1,50,32]{1,2,0:T(8,128)S(1)}, f32[1,50,32]{1,2,0:T(8,128)}, u32[]{:S(2)}) copy-start(f32[1,50,32]{1,2,0:T(8,128)} %param.16) | copy-start | bytes 19204
  270.8 32.2 %copy-start.46 = (f32[1024]{0:T(1024)S(1)}, f32[1024]{0:T(1024)}, u32[]{:S(2)}) copy-start(f32[1024]{0:T(1024)} %param.26) | copy-start | bytes 12292
  270.8 32.4 %copy-start.52 = (f32[1024]{0:T(1024)S(1)}, f32[1024]{0:T(1024)}, u32[]{:S(2)}) copy-start(f32[1024]{0:T(1024)} %pad_maximum_fusion.2) | copy-start | bytes 12292
  271.1 32.7 %copy-start.42 = (f32[1024]{0:T(1024)S(1)}, f32[1024]{0:T(1024)}, u32[]{:S(2)}) copy-start(f32[1024]{0:T(1024)} %param.21) | copy-start | bytes 12292
  271.1 33.4 %copy-start.1 = (bf16[1024,1024]{1,0:T(8,128)(2,1)S(1)}, bf16[1024,1024]{1,0:T(8,128)(2,1)}, u32[]{:S(2)}) copy-start(bf16[1024,1024]{1,0:T(8,128)(2,1)} %all-gather.8.cloned.1.call-done) | copy-start | bytes 6291460
  303.2 1.8 copy-start.8
  303.2 1.8 copy-start.13
  304.4 3.2 copy-start.25
  304.9 2.7 copy-start.4
  310.2 7.4 %copy-start.3 = (bf16[1024,512]{1,0:T(8,128)(2,1)S(1)}, bf16[1024,512]{1,0:T(8,128)(2,1)}, u32[]{:S(2)}) copy-start(bf16[1024,512]{1,0:T(8,128)(2,1)} %all-gather.12.cloned.1.call-done) | copy-start | bytes 3145732
  310.2 7.4 %copy-start.26 = (bf16[50,1024]{1,0:T(8,128)(2,1)S(1)}, bf16[50,1024]{1,0:T(8,128)(2,1)}, u32[]{:S(2)}) copy-start(bf16[50,1024]{1,0:T(8,128)(2,1)} %copy-done.25) | copy-start | bytes 307204
  313.3 2.0 copy-start.37
  315.4 2.1 copy-start.57
  323.6 2.3 copy-start.31
  323.6 2.3 copy-start.47
  323.6 2.5 copy-start.51
  323.6 3.7 %copy-start.43 = (f32[1024]{0:T(1024)S(1)}, f32[1024]{0:T(1024)}, u32[]{:S(2)}) copy-start(f32[1024]{0:T(1024)} %param.21) | copy-start | bytes 12292
  326.1 1.9 copy-start.40
  326.2 1.9 copy-start.9
  326.2 1.9 copy-start.14
  327.4 2.7 copy-start.27
  327.9 2.2 copy-start.5
  332.6 6.7 %copy-start.28 = (bf16[50,1024]{1,0:T(8,128)(2,1)S(1)}, bf16[50,1024]{1,0:T(8,128)(2,1)}, u32[]{:S(2)}) copy-start(bf16[50,1024]{1,0:T(8,128)(2,1)} %copy-done.27) | copy-start | bytes 307204
  345.3 2.2 copy-start.32
  348.5 3.3 copy-start.10
  348.5 3.3 copy-start.15
  351.8 1.6 copy-start.11
  351.9 1.6 copy-start.16
  353.3 3.4 copy-start.24
  354.5 5.5 %copy-start.2 = (bf16[1024,1024]{1,0:T(8,128)(2,1)S(1)}, bf16[1024,1024]{1,0:T(8,128)(2,1)}, u32[]{:S(2)}) copy-start(bf16[1024,1024]{1,0:T(8,128)(2,1)} %all-gather.14.cloned.1.call-done) | copy-start | bytes 6291460
  354.5 5.5 %copy-start.20 = (f32[50,1024]{1,0:T(8,128)S(1)}, f32[50,1024]{1,0:T(8,128)}, u32[]{:S(2)}) copy-start(f32[50,1024]{1,0:T(8,128)} %copy-done.19) | copy-start | bytes 614404
  357.6 2.9 copy-start.33
  357.6 2.9 copy-start.48
  (16 other events, 17.1 us)
Sparse Core Ops, SparseCore 0:
  9.5 40.6 all-gather.9
  52.4 36.8 all-gather.11
  91.4 40.4 all-gather.7
  133.9 125.1 all-gather.5
  261.1 39.6 all-gather.13
where the time goes:
time: 369 us; the launch traced here: 368 us
  waiting for transfers between devices  266 us (72%)
  matrix products  50.5 us (14%)
  local copies, waits for them, and re-layouts  20.1 us (5%)
  other arithmetic  16.4 us (4%)
  between operations  15.1 us (4%)
    all_gather x1, waiting for transfers between devices, shards(): lax.all_gather(stacked, 'wide', axis=1, tiled=True)  124 us
    all_gather x1, waiting for transfers between devices, shards(): lax.all_gather(expert_query, 'wide', axis=0, tiled=True)  40.4 us
    all_gather x1, waiting for transfers between devices, shards(): lax.all_gather(expert_value, 'wide', axis=0, tiled=True)  37.4 us
    all_gather x1, waiting for transfers between devices, shards(): lax.all_gather(expert_key, 'wide', axis=0, tiled=True)  31.2 us
    all_gather x1, waiting for transfers between devices, shards(): lax.all_gather(expert_output, 'wide', axis=0, tiled=True)  29.5 us
    dot_general x1, matrix products, shards(): jnp.einsum('pd,kdc->pkc', normed, lax.all_gather(stacked, 'wide', axis=1,...  9.54 us
  transfers between devices with their start and end apart: 5, of which 5 were waited for; matrix products, arithmetic and copies ran while one was open for 7% of the time, Pallas kernels for 0%

commit v1 on v0

--- a/solution.py
+++ b/solution.py
@@ -1,3 +1,4 @@
+import functools
 import jax
 import jax.numpy as jnp
 from jax import lax
@@ -7,6 +8,33 @@
 STEPS = 4
 rope_base = 1000000.0
 norm_eps = 1e-06
+
+
+def cover_lines_all(x_in, bus_axis, dimension_no):
+    main = jax.lax.axis_size(bus_axis)
+    odd, b_now, f_now = (main, jax.lax.axis_index(bus_axis), x_in.shape[dimension_no])
+    column = [dev_i * odd if k0 == dimension_no else dev_i for k0, dev_i in enumerate(x_in.shape)]
+    piece_out = jnp.zeros(column, x_in.dtype)
+    a_next = out_arr = x_in
+    it = 1
+    base_arr = lax.dynamic_update_slice_in_dim(piece_out, x_in, b_now * f_now, axis=dimension_no)
+    while it < odd // 2 + 1:
+        a_next = jax.lax.ppermute(a_next, bus_axis, [(k0, (k0 + 1) % odd) for k0 in range(odd)])
+        base_arr = lax.dynamic_update_slice_in_dim(
+            base_arr, a_next, (b_now - it) % odd * f_now, axis=dimension_no
+        )
+        if 2 * it < odd:
+            out_arr = jax.lax.ppermute(
+                out_arr, bus_axis, [(k0, (k0 - 1) % odd) for k0 in range(odd)]
+            )
+            base_arr = lax.dynamic_update_slice_in_dim(
+                base_arr, out_arr, (b_now + it) % odd * f_now, axis=dimension_no
+            )
+        it += 1
+    return base_arr
+
+
+bring_group = functools.partial(cover_lines_all, bus_axis="wide", dimension_no=0)
 
 
 def normalize(values, norm_gain):
@@ -134,7 +162,7 @@
         lax.all_gather(expert_query, "wide", axis=0, tiled=True),
         lax.all_gather(expert_key, "wide", axis=0, tiled=True),
         lax.all_gather(expert_value, "wide", axis=0, tiled=True),
-        lax.all_gather(expert_output, "wide", axis=0, tiled=True),
+        bring_group(expert_output),
     )
     hidden = prefix_hidden[0]
     row_count = hidden.shape[0]

time: 369 us -> 344 us (0.932)
  waiting for transfers between devices: 266 us -> 204 us
  starting transfers between devices: 0.16 us -> 32.4 us
  other arithmetic: 16.4 us -> 20.1 us
    ppermute x0 -> x15, starting transfers between devices: none -> 32.3 us  [the longest x7 31.7 us: cover_lines_all(): jax.lax.ppermute(out_arr, bus_axis, [(k0, (k0 - 1) % odd) for k0 in range...]
    all_gather x1, waiting for transfers between devices: 31.2 us -> 0.02 us  [shards(): lax.all_gather(expert_key, 'wide', axis=0, tiled=True)]
    all_gather x1 -> x0, waiting for transfers between devices: 29.5 us -> none  [shards(): lax.all_gather(expert_output, 'wide', axis=0, tiled=True)]
    ppermute x0 -> x15, waiting for transfers between devices: none -> 23.9 us  [the longest x8 23.9 us: cover_lines_all(): jax.lax.ppermute(a_next, bus_axis, [(k0, (k0 + 1) % odd) for k0 in range(...]
    all_gather x1, waiting for transfers between devices: 37.4 us -> 13.8 us  [shards(): lax.all_gather(expert_value, 'wide', axis=0, tiled=True)]
  transfers between devices with their start and end apart: 5 -> 19, of which waited for: 5 -> 10; matrix products, arithmetic and copies ran while one was open for 7% -> 5% of each run, Pallas kernels for 0% -> 0%
where the time goes in v1:
time: 344 us; the launch traced here: 343 us
  waiting for transfers between devices  204 us (59%)
  matrix products  51.9 us (15%)
  starting transfers between devices  32.4 us (9%)
  other arithmetic  20.1 us (6%)
  local copies, waits for them, and re-layouts  18.7 us (5%)
  between operations  15.5 us (5%)
    all_gather x1, waiting for transfers between devices, shards(): lax.all_gather(stacked, 'wide', axis=1, tiled=True)  124 us
    all_gather x1, waiting for transfers between devices, shards(): lax.all_gather(expert_query, 'wide', axis=0, tiled=True)  40.3 us
    ppermute x7, starting transfers between devices, cover_lines_all(): jax.lax.ppermute(out_arr, bus_axis, [(k0, (k0 - 1) % odd) for k0 in range...  31.7 us
    ppermute x8, waiting for transfers between devices, cover_lines_all(): jax.lax.ppermute(a_next, bus_axis, [(k0, (k0 + 1) % odd) for k0 in range(...  23.9 us
    all_gather x1, waiting for transfers between devices, shards(): lax.all_gather(expert_value, 'wide', axis=0, tiled=True)  13.8 us
    dot_general x1, matrix products, shards(): jnp.einsum('pd,kdc->pkc', normed, lax.all_gather(stacked, 'wide', axis=1,...  9.61 us
    dot_general x4, matrix products, attend(): jnp.einsum('grcp,pgh->cgrh', prefix_prob, prefix_values, preferred_elemen...  7.67 us
  transfers between devices with their start and end apart: 19, of which 10 were waited for; matrix products, arithmetic and copies ran while one was open for 5% of the time, Pallas kernels for 0%

profile of v1, /device:TPU:0, one launch (start us, length us, event | category | flops | bytes accessed | tf_op | source)
XLA Modules:
  0.0 342.7 jit_solution(7726771379037573603)
XLA Ops:
  8.8 2.3 pad_maximum_fusion
  11.7 5.0 %collective-permute-start.1 = (bf16[64,1024]{1,0:T(8,128)(2,1)S(1)}, bf16[64,1024]{1,0:T(8,128)(2,1)S(1)}, u32[]{:S(2)}, u32[]{:S(2)}) collective-permute-start(bf16[64,1024]{1,0:T(8,128)(2,1)S(1)} %copy-done.42), channel_id=1, source_target_pairs={{0,15},{1,0},{2,1},{3,2},{4,3},{5,4},{6,5},{7,6},{8,7},{9,8},{10,9... | collective-permute-start | bytes 393224 | tf_op jit(solution)/shard_map/ppermute | solution.py:27
  20.0 3.2 fusion
  23.4 1.2 fusion.47
  25.4 4.4 %collective-permute-start.3 = (bf16[64,1024]{1,0:T(8,128)(2,1)S(1)}, bf16[64,1024]{1,0:T(8,128)(2,1)S(1)}, u32[]{:S(2)}, u32[]{:S(2)}) collective-permute-start(bf16[64,1024]{1,0:T(8,128)(2,1)S(1)} %collective-permute-done.1), channel_id=1, source_target_pairs={{0,15},{1,0},{2,1},{3,2},{4,3},{5,4},{6,5},{7,6},{8,7},{9,8},{10,9... | collective-permute-start | bytes 393224 | tf_op jit(solution)/shard_map/ppermute | solution.py:27
  29.9 2.8 collective-permute-done.2
  32.7 4.4 %collective-permute-start.5 = (bf16[64,1024]{1,0:T(8,128)(2,1)S(1)}, bf16[64,1024]{1,0:T(8,128)(2,1)S(1)}, u32[]{:S(2)}, u32[]{:S(2)}) collective-permute-start(bf16[64,1024]{1,0:T(8,128)(2,1)S(1)} %collective-permute-done.3), channel_id=1, source_target_pairs={{0,15},{1,0},{2,1},{3,2},{4,3},{5,4},{6,5},{7,6},{8,7},{9,8},{10,9... | collective-permute-start | bytes 393224 | tf_op jit(solution)/shard_map/ppermute | solution.py:27
  37.2 2.7 collective-permute-done.4
  39.9 4.5 %collective-permute-start.7 = (bf16[64,1024]{1,0:T(8,128)(2,1)S(1)}, bf16[64,1024]{1,0:T(8,128)(2,1)S(1)}, u32[]{:S(2)}, u32[]{:S(2)}) collective-permute-start(bf16[64,1024]{1,0:T(8,128)(2,1)S(1)} %collective-permute-done.5), channel_id=1, source_target_pairs={{0,15},{1,0},{2,1},{3,2},{4,3},{5,4},{6,5},{7,6},{8,7},{9,8},{10,9... | collective-permute-start | bytes 393224 | tf_op jit(solution)/shard_map/ppermute | solution.py:27
  44.4 2.9 collective-permute-done.6
  47.3 4.4 %collective-permute-start.9 = (bf16[64,1024]{1,0:T(8,128)(2,1)S(1)}, bf16[64,1024]{1,0:T(8,128)(2,1)S(1)}, u32[]{:S(2)}, u32[]{:S(2)}) collective-permute-start(bf16[64,1024]{1,0:T(8,128)(2,1)S(1)} %collective-permute-done.7), channel_id=1, source_target_pairs={{0,15},{1,0},{2,1},{3,2},{4,3},{5,4},{6,5},{7,6},{8,7},{9,8},{10,9... | collective-permute-start | bytes 393224 | tf_op jit(solution)/shard_map/ppermute | solution.py:27
  51.8 2.7 collective-permute-done.8
  54.5 4.4 %collective-permute-start.11 = (bf16[64,1024]{1,0:T(8,128)(2,1)S(1)}, bf16[64,1024]{1,0:T(8,128)(2,1)S(1)}, u32[]{:S(2)}, u32[]{:S(2)}) collective-permute-start(bf16[64,1024]{1,0:T(8,128)(2,1)S(1)} %collective-permute-done.9), channel_id=1, source_target_pairs={{0,15},{1,0},{2,1},{3,2},{4,3},{5,4},{6,5},{7,6},{8,7},{9,8},{10,9... | collective-permute-start | bytes 393224 | tf_op jit(solution)/shard_map/ppermute | solution.py:27
  59.0 2.7 collective-permute-done.10
  61.7 4.4 %collective-permute-start.13 = (bf16[64,1024]{1,0:T(8,128)(2,1)S(1)}, bf16[64,1024]{1,0:T(8,128)(2,1)S(1)}, u32[]{:S(2)}, u32[]{:S(2)}) collective-permute-start(bf16[64,1024]{1,0:T(8,128)(2,1)S(1)} %collective-permute-done.11), channel_id=1, source_target_pairs={{0,15},{1,0},{2,1},{3,2},{4,3},{5,4},{6,5},{7,6},{8,7},{9,8},{10,9... | collective-permute-start | bytes 393224 | tf_op jit(solution)/shard_map/ppermute | solution.py:27
  66.2 3.1 collective-permute-done.12
  69.3 7.0 %collective-permute-done.14 = bf16[64,1024]{1,0:T(8,128)(2,1)S(1)} collective-permute-done((bf16[64,1024]{1,0:T(8,128)(2,1)S(1)}, bf16[64,1024]{1,0:T(8,128)(2,1)S(1)}, u32[]{:S(2)}, u32[]{:S(2)}) %collective-permute-start.14) | collective-permute-done | bytes 131104 | tf_op jit(solution)/shard_map/ppermute | solution.py:22
  76.4 1.5 fusion.107
  77.9 13.8 %all-gather.11.cloned.1.call-done = bf16[1024,512]{1,0:T(8,128)(2,1)} async-done(((bf16[64,512]{1,0:T(8,128)(2,1)}), bf16[1024,512]{1,0:T(8,128)(2,1)}) %all-gather.11.cloned.1.call-update) | async-done | bytes 1048592 | tf_op jit(solution)/shard_map/all_gather | solution.py:164
  91.7 1.5 convolution_convert_fusion.3
  94.0 40.3 %all-gather.7.cloned.1.call-done = bf16[1024,1024]{1,0:T(8,128)(2,1)} async-done(((bf16[64,1024]{1,0:T(8,128)(2,1)}), bf16[1024,1024]{1,0:T(8,128)(2,1)}) %all-gather.7.cloned.1.call-update) | async-done | bytes 2097168 | tf_op jit(solution)/shard_map/all_gather | solution.py:162
  134.3 2.1 fusion.106
  137.8 123.8 %all-gather.5.cloned.1.call-done = bf16[2,8192,512]{2,1,0:T(8,128)(2,1)} async-done(((bf16[2,512,512]{2,1,0:T(8,128)(2,1)}), bf16[2,8192,512]{2,1,0:T(8,128)(2,1)}) %all-gather.5.cloned.1.call-update) | async-done | bytes 16777232 | tf_op jit(solution)/shard_map/all_gather | solution.py:174
  261.6 9.6 %fusion.4 = f32[256,2,512]{2,0,1:T(8,128)S(1)} fusion(bf16[2,8192,512]{2,1,0:T(8,128)(2,1)} %all-gather.5.cloned.1.call-done, bf16[1,256,8192]{2,1,0:T(8,128)(2,1)} %param.14, f32[8192]{0:T(1024)S(1)} %copy-done.61, f32[256]{0:T(256)S(1)} %add_rsqrt_fusion), kind=kOutput, calls=%fused_computation.6 | convolution fusion | flops 4303355904 | bytes 22053888 | tf_op jit(solution)/shard_map/pd,kdc->pkc/dot_general | solution.py:171
  272.5 1.2 subtract_convert_fusion
  275.4 1.3 fusion.30
  281.2 1.7 fusion.100
  285.8 1.2 fusion.101
  287.7 1.3 fusion.27
  289.1 2.1 fusion.31
  292.2 1.4 reshape.312
  293.6 1.3 fusion.19
  295.7 1.6 convert_element_type.174
  297.3 1.7 multiply_reduce_fusion.4
  303.6 1.6 reshape.314
  307.1 1.2 fusion.103
  308.3 1.4 fusion.28
  309.7 2.1 fusion.32
  312.8 1.4 reshape.315
  314.2 1.3 fusion.18
  316.3 1.6 convert_element_type.184
  317.9 1.7 multiply_reduce_fusion.2
  320.6 1.2 multiply_reduce_fusion.1
  323.6 1.7 fusion.104
  326.6 1.2 fusion.105
  327.8 1.3 fusion.29
  329.2 2.1 fusion.33
  333.2 1.3 fusion.17
  (271 shorter events, 36.3 us)
Async XLA Ops:
  6.5 13.0 %copy-start = (f32[32,1024]{1,0:T(8,128)S(1)}, f32[32,1024]{1,0:T(8,128)}, u32[]{:S(2)}) copy-start(f32[32,1024]{1,0:T(8,128)} %param.20) | copy-start | bytes 393220
  6.5 4.6 %copy-start.42 = (bf16[64,1024]{1,0:T(8,128)(2,1)S(1)}, bf16[64,1024]{1,0:T(8,128)(2,1)}, u32[]{:S(2)}) copy-start(bf16[64,1024]{1,0:T(8,128)(2,1)} %param.25) | copy-start | bytes 393220
  6.5 12.9 %copy-start.45 = (f32[1,50,32]{1,2,0:T(8,128)S(1)}, f32[1,50,32]{1,2,0:T(8,128)}, u32[]{:S(2)}) copy-start(f32[1,50,32]{1,2,0:T(8,128)} %param.16) | copy-start | bytes 19204
  6.5 69.8 %all-gather.9.cloned.1.call-start = ((), (), s32[]{:S(2)}) async-start(), calls=%async_computation.2 | async-start | bytes 1114112 | tf_op jit(solution)/shard_map/all_gather | solution.py:163
  7.3 84.4 %all-gather.11.cloned.1.call-start = ((), (), s32[]{:S(2)}) async-start(), calls=%async_computation.3 | async-start | bytes 1114112 | tf_op jit(solution)/shard_map/all_gather | solution.py:164
  8.0 126.3 %all-gather.7.cloned.1.call-start = ((), (), s32[]{:S(2)}) async-start(), calls=%async_computation.1 | async-start | bytes 2228224 | tf_op jit(solution)/shard_map/all_gather | solution.py:162
  8.7 252.8 %all-gather.5.cloned.1.call-start = ((), (), s32[]{:S(2)}) async-start(), calls=%async_computation | async-start | bytes 17825792 | tf_op jit(solution)/shard_map/all_gather | solution.py:174
  11.1 14.2 %collective-permute-start = (bf16[64,1024]{1,0:T(8,128)(2,1)S(1)}, bf16[64,1024]{1,0:T(8,128)(2,1)S(1)}, u32[]{:S(2)}, u32[]{:S(2)}) collective-permute-start(bf16[64,1024]{1,0:T(8,128)(2,1)S(1)} %copy-done.42), channel_id=1, source_target_pairs={{0,1},{1,2},{2,3},{3,4},{4,5},{5,6},{6,7},{7,8},{8,9},{9,10},{10,1... | collective-permute-start | bytes 393224 | tf_op jit(solution)/shard_map/ppermute | solution.py:22
  11.7 13.7 %collective-permute-start.1 = (bf16[64,1024]{1,0:T(8,128)(2,1)S(1)}, bf16[64,1024]{1,0:T(8,128)(2,1)S(1)}, u32[]{:S(2)}, u32[]{:S(2)}) collective-permute-start(bf16[64,1024]{1,0:T(8,128)(2,1)S(1)} %copy-done.42), channel_id=1, source_target_pairs={{0,15},{1,0},{2,1},{3,2},{4,3},{5,4},{6,5},{7,6},{8,7},{9,8},{10,9... | collective-permute-start | bytes 393224 | tf_op jit(solution)/shard_map/ppermute | solution.py:27
  20.0 4.7 %copy-start.14 = (f32[50,1024]{1,0:T(8,128)}, f32[50,1024]{1,0:T(8,128)S(1)}, u32[]{:S(2)}) copy-start(f32[50,1024]{1,0:T(8,128)S(1)} %get-tuple-element.38) | copy-start | bytes 614404
  20.0 4.7 %copy-start.43 = (f32[1024]{0:T(1024)S(1)}, f32[1024]{0:T(1024)}, u32[]{:S(2)}) copy-start(f32[1024]{0:T(1024)} %param.21) | copy-start | bytes 12292
  23.4 256.8 %copy-start.8 = (f32[50,64]{1,0:T(8,128)}, f32[50,64]{1,0:T(8,128)S(1)}, u32[]{:S(2)}) copy-start(f32[50,64]{1,0:T(8,128)S(1)} %get-tuple-element.33) | copy-start | bytes 38404
  23.4 256.8 %copy-start.11 = (f32[50,64]{1,0:T(8,128)}, f32[50,64]{1,0:T(8,128)S(1)}, u32[]{:S(2)}) copy-start(f32[50,64]{1,0:T(8,128)S(1)} %get-tuple-element.34) | copy-start | bytes 38404
  24.8 249.1 %copy-start.55 = (pred[256]{0:T(512)(128)(4,1)}, pred[256]{0:T(512)(128)(4,1)S(1)}, u32[]{:S(2)}) copy-start(pred[256]{0:T(512)(128)(4,1)S(1)} %iota_compare_fusion) | copy-start | bytes 772
  25.4 7.4 %collective-permute-start.2 = (bf16[64,1024]{1,0:T(8,128)(2,1)S(1)}, bf16[64,1024]{1,0:T(8,128)(2,1)S(1)}, u32[]{:S(2)}, u32[]{:S(2)}) collective-permute-start(bf16[64,1024]{1,0:T(8,128)(2,1)S(1)} %collective-permute-done), channel_id=1, source_target_pairs={{0,1},{1,2},{2,3},{3,4},{4,5},{5,6},{6,7},{7,8},{8,9},{9,10},{10,1... | collective-permute-start | bytes 393224 | tf_op jit(solution)/shard_map/ppermute | solution.py:22
  25.4 7.3 %collective-permute-start.3 = (bf16[64,1024]{1,0:T(8,128)(2,1)S(1)}, bf16[64,1024]{1,0:T(8,128)(2,1)S(1)}, u32[]{:S(2)}, u32[]{:S(2)}) collective-permute-start(bf16[64,1024]{1,0:T(8,128)(2,1)S(1)} %collective-permute-done.1), channel_id=1, source_target_pairs={{0,15},{1,0},{2,1},{3,2},{4,3},{5,4},{6,5},{7,6},{8,7},{9,8},{10,9... | collective-permute-start | bytes 393224 | tf_op jit(solution)/shard_map/ppermute | solution.py:27
  32.7 7.2 %collective-permute-start.4 = (bf16[64,1024]{1,0:T(8,128)(2,1)S(1)}, bf16[64,1024]{1,0:T(8,128)(2,1)S(1)}, u32[]{:S(2)}, u32[]{:S(2)}) collective-permute-start(bf16[64,1024]{1,0:T(8,128)(2,1)S(1)} %collective-permute-done.2), channel_id=1, source_target_pairs={{0,1},{1,2},{2,3},{3,4},{4,5},{5,6},{6,7},{7,8},{8,9},{9,10},{10,1... | collective-permute-start | bytes 393224 | tf_op jit(solution)/shard_map/ppermute | solution.py:22
  32.7 7.2 %collective-permute-start.5 = (bf16[64,1024]{1,0:T(8,128)(2,1)S(1)}, bf16[64,1024]{1,0:T(8,128)(2,1)S(1)}, u32[]{:S(2)}, u32[]{:S(2)}) collective-permute-start(bf16[64,1024]{1,0:T(8,128)(2,1)S(1)} %collective-permute-done.3), channel_id=1, source_target_pairs={{0,15},{1,0},{2,1},{3,2},{4,3},{5,4},{6,5},{7,6},{8,7},{9,8},{10,9... | collective-permute-start | bytes 393224 | tf_op jit(solution)/shard_map/ppermute | solution.py:27
  39.9 7.4 %collective-permute-start.6 = (bf16[64,1024]{1,0:T(8,128)(2,1)S(1)}, bf16[64,1024]{1,0:T(8,128)(2,1)S(1)}, u32[]{:S(2)}, u32[]{:S(2)}) collective-permute-start(bf16[64,1024]{1,0:T(8,128)(2,1)S(1)} %collective-permute-done.4), channel_id=1, source_target_pairs={{0,1},{1,2},{2,3},{3,4},{4,5},{5,6},{6,7},{7,8},{8,9},{9,10},{10,1... | collective-permute-start | bytes 393224 | tf_op jit(solution)/shard_map/ppermute | solution.py:22
  39.9 7.4 %collective-permute-start.7 = (bf16[64,1024]{1,0:T(8,128)(2,1)S(1)}, bf16[64,1024]{1,0:T(8,128)(2,1)S(1)}, u32[]{:S(2)}, u32[]{:S(2)}) collective-permute-start(bf16[64,1024]{1,0:T(8,128)(2,1)S(1)} %collective-permute-done.5), channel_id=1, source_target_pairs={{0,15},{1,0},{2,1},{3,2},{4,3},{5,4},{6,5},{7,6},{8,7},{9,8},{10,9... | collective-permute-start | bytes 393224 | tf_op jit(solution)/shard_map/ppermute | solution.py:27
  47.3 7.2 %collective-permute-start.8 = (bf16[64,1024]{1,0:T(8,128)(2,1)S(1)}, bf16[64,1024]{1,0:T(8,128)(2,1)S(1)}, u32[]{:S(2)}, u32[]{:S(2)}) collective-permute-start(bf16[64,1024]{1,0:T(8,128)(2,1)S(1)} %collective-permute-done.6), channel_id=1, source_target_pairs={{0,1},{1,2},{2,3},{3,4},{4,5},{5,6},{6,7},{7,8},{8,9},{9,10},{10,1... | collective-permute-start | bytes 393224 | tf_op jit(solution)/shard_map/ppermute | solution.py:22
  47.3 7.2 %collective-permute-start.9 = (bf16[64,1024]{1,0:T(8,128)(2,1)S(1)}, bf16[64,1024]{1,0:T(8,128)(2,1)S(1)}, u32[]{:S(2)}, u32[]{:S(2)}) collective-permute-start(bf16[64,1024]{1,0:T(8,128)(2,1)S(1)} %collective-permute-done.7), channel_id=1, source_target_pairs={{0,15},{1,0},{2,1},{3,2},{4,3},{5,4},{6,5},{7,6},{8,7},{9,8},{10,9... | collective-permute-start | bytes 393224 | tf_op jit(solution)/shard_map/ppermute | solution.py:27
  54.5 7.2 %collective-permute-start.10 = (bf16[64,1024]{1,0:T(8,128)(2,1)S(1)}, bf16[64,1024]{1,0:T(8,128)(2,1)S(1)}, u32[]{:S(2)}, u32[]{:S(2)}) collective-permute-start(bf16[64,1024]{1,0:T(8,128)(2,1)S(1)} %collective-permute-done.8), channel_id=1, source_target_pairs={{0,1},{1,2},{2,3},{3,4},{4,5},{5,6},{6,7},{7,8},{8,9},{9,10},{10,1... | collective-permute-start | bytes 393224 | tf_op jit(solution)/shard_map/ppermute | solution.py:22
  54.5 7.2 %collective-permute-start.11 = (bf16[64,1024]{1,0:T(8,128)(2,1)S(1)}, bf16[64,1024]{1,0:T(8,128)(2,1)S(1)}, u32[]{:S(2)}, u32[]{:S(2)}) collective-permute-start(bf16[64,1024]{1,0:T(8,128)(2,1)S(1)} %collective-permute-done.9), channel_id=1, source_target_pairs={{0,15},{1,0},{2,1},{3,2},{4,3},{5,4},{6,5},{7,6},{8,7},{9,8},{10,9... | collective-permute-start | bytes 393224 | tf_op jit(solution)/shard_map/ppermute | solution.py:27
  61.7 7.6 %collective-permute-start.12 = (bf16[64,1024]{1,0:T(8,128)(2,1)S(1)}, bf16[64,1024]{1,0:T(8,128)(2,1)S(1)}, u32[]{:S(2)}, u32[]{:S(2)}) collective-permute-start(bf16[64,1024]{1,0:T(8,128)(2,1)S(1)} %collective-permute-done.10), channel_id=1, source_target_pairs={{0,1},{1,2},{2,3},{3,4},{4,5},{5,6},{6,7},{7,8},{8,9},{9,10},{10,1... | collective-permute-start | bytes 393224 | tf_op jit(solution)/shard_map/ppermute | solution.py:22
  61.7 7.6 %collective-permute-start.13 = (bf16[64,1024]{1,0:T(8,128)(2,1)S(1)}, bf16[64,1024]{1,0:T(8,128)(2,1)S(1)}, u32[]{:S(2)}, u32[]{:S(2)}) collective-permute-start(bf16[64,1024]{1,0:T(8,128)(2,1)S(1)} %collective-permute-done.11), channel_id=1, source_target_pairs={{0,15},{1,0},{2,1},{3,2},{4,3},{5,4},{6,5},{7,6},{8,7},{9,8},{10,9... | collective-permute-start | bytes 393224 | tf_op jit(solution)/shard_map/ppermute | solution.py:27
  69.2 7.1 %collective-permute-start.14 = (bf16[64,1024]{1,0:T(8,128)(2,1)S(1)}, bf16[64,1024]{1,0:T(8,128)(2,1)S(1)}, u32[]{:S(2)}, u32[]{:S(2)}) collective-permute-start(bf16[64,1024]{1,0:T(8,128)(2,1)S(1)} %collective-permute-done.12), channel_id=1, source_target_pairs={{0,1},{1,2},{2,3},{3,4},{4,5},{5,6},{6,7},{7,8},{8,9},{9,10},{10,1... | collective-permute-start | bytes 393224 | tf_op jit(solution)/shard_map/ppermute | solution.py:22
  94.0 167.6 %copy-start.61 = (f32[8192]{0:T(1024)S(1)}, f32[8192]{0:T(1024)}, u32[]{:S(2)}) copy-start(f32[8192]{0:T(1024)} %param.17) | copy-start | bytes 98308
  136.8 134.4 %copy-start.31 = (bf16[50,8,128]{2,0,1:T(8,128)(2,1)}, bf16[50,8,128]{2,0,1:T(8,128)(2,1)S(1)}, u32[]{:S(2)}) copy-start(bf16[50,8,128]{2,0,1:T(8,128)(2,1)S(1)} %copy.37) | copy-start | bytes 307204
  274.6 3.4 copy-start.15
  279.6 3.2 copy-start.22
  280.1 2.8 copy-start.5
  283.8 7.4 %copy-start.4 = (bf16[1024,512]{1,0:T(8,128)(2,1)S(1)}, bf16[1024,512]{1,0:T(8,128)(2,1)}, u32[]{:S(2)}) copy-start(bf16[1024,512]{1,0:T(8,128)(2,1)} %all-gather.11.cloned.1.call-done) | copy-start | bytes 3145732
  283.8 7.4 %copy-start.23 = (bf16[50,1024]{1,0:T(8,128)(2,1)S(1)}, bf16[50,1024]{1,0:T(8,128)(2,1)}, u32[]{:S(2)}) copy-start(bf16[50,1024]{1,0:T(8,128)(2,1)} %copy-done.22) | copy-start | bytes 307204
  297.3 2.6 copy-start.44
  297.3 2.7 copy-start.2
  300.0 2.7 copy-start.24
  305.2 6.7 %copy-start.25 = (bf16[50,1024]{1,0:T(8,128)(2,1)S(1)}, bf16[50,1024]{1,0:T(8,128)(2,1)}, u32[]{:S(2)}) copy-start(bf16[50,1024]{1,0:T(8,128)(2,1)} %copy-done.24) | copy-start | bytes 307204
  317.9 4.8 %copy-start.3 = (bf16[1024,1024]{1,0:T(8,128)(2,1)S(1)}, bf16[1024,1024]{1,0:T(8,128)(2,1)}, u32[]{:S(2)}) copy-start(bf16[1024,1024]{1,0:T(8,128)(2,1)} %all-gather.7.cloned.1.call-done) | copy-start | bytes 6291460
  320.6 2.7 copy-start.10
  320.6 2.7 copy-start.13
  322.7 2.6 copy-start.20
  325.3 2.5 copy-start.52
  325.6 5.8 %copy-start.21 = (bf16[50,1024]{1,0:T(8,128)(2,1)S(1)}, bf16[50,1024]{1,0:T(8,128)(2,1)}, u32[]{:S(2)}) copy-start(bf16[50,1024]{1,0:T(8,128)(2,1)} %copy-done.20) | copy-start | bytes 307204
  327.8 3.6 %copy-start.50 = (f32[4,2,50]{2,1,0:T(2,128)}, f32[4,2,50]{2,1,0:T(2,128)S(1)}, u32[]{:S(2)}) copy-start(f32[4,2,50]{2,1,0:T(2,128)S(1)} %max.31) | copy-start | bytes 4804
  329.2 5.4 %copy-start.17 = (f32[50,1024]{1,0:T(8,128)S(1)}, f32[50,1024]{1,0:T(8,128)}, u32[]{:S(2)}) copy-start(f32[50,1024]{1,0:T(8,128)} %copy-done.16) | copy-start | bytes 614404
  332.3 2.9 copy-start.30
  332.3 2.9 copy-start.49
  (33 other events, 52.4 us)
Sparse Core Ops, SparseCore 0:
  9.5 42.8 all-gather.8
  54.5 37.1 all-gather.10
  93.9 40.4 all-gather.6
  136.4 125.1 all-gather.4
